TPU v7x, 256 devices: a whole 4x4x8 slice. The times are simulated.
256 devices in a mesh: row: 16 (over y, z_hi), col: 16 (over x, z_lo, core).
Axes of the slice: x: 4, y: 4, z: 8 (z_hi: 4, z_lo: 2; z = z_hi * 2 + z_lo), core: 2. Of those that a mesh axis runs over, the one named last changes fastest.
Arguments:
- fit_tiles: bfloat16 [32, 96, 128, 128], P('row', 'col'), may hold values from -6 to 6
- aux_list: int32 [32, 96], P('row', 'col'), may hold values from 0 to 11, as said below
- aux_count: int32 [32, 16], P('row', 'col'), may hold values from 1 to 6, as said below
- metric: bfloat16 [192, 128, 128], P('col', 'row'), may hold values from -0.5 to 0.5
Outputs:
- exchange: float32 [4096, 4096], P('col', 'row')
Inputs may be any that keep to these rules, and one draw needn't show every extreme that they name: `aux_list`: within one atom block and one col shard, the first 6 slots name distinct auxiliary blocks. `aux_count`: counts follow a density per atom block; the largest is reached in every draw.
All inputs are finite; a program needn't handle non-finite values.
Results may differ from a plain program's by a relative error of at most 0.0015.
Values may be sent and summed in bfloat16 or wider, within the bound.
No kernel may reach another device: no remote copies, remote signals or barrier semaphores. Data moves between devices by JAX's collectives and lax.ppermute only.
A program may use at most 64 MiB of HBM per device.

v0:
```python
import functools

import jax
import jax.numpy as jnp
from jax import lax
from jax.experimental import pallas as pl
from jax.experimental.pallas import tpu as pltpu
from jax.sharding import Mesh, PartitionSpec as P


AUXB = 128
BS = 128
QS = 6
QB = 12
NA = 2
ROWS = NA * BS
WIDE = (QB + 1) * AUXB
USED = QB * AUXB
MROWS = 8
HALF = QS * BS
PART = QB * MROWS
LIST0 = 4 * PART
SMALL = LIST0 + 16
F32 = jnp.float32
BF16 = jnp.bfloat16

SMEM = pl.BlockSpec(memory_space=pltpu.SMEM)
VMEM = pl.BlockSpec(memory_space=pltpu.VMEM)
PARAMS = pltpu.CompilerParams(vmem_limit_bytes=14 << 20)


def ring(n, k):
    return [(i, (i + k) % n) for i in range(n)]


def back(i, k):
    return lax.rem(i - k + 4, 4)


def pack_kernel(lists, counts, metric, out):
    out[0:PART, :] = metric[...]
    slot = lax.broadcasted_iota(jnp.int32, (NA, QS), 1)
    marked = jnp.where(slot < counts[...], lists[...], QB)
    tail = jnp.concatenate([marked, jnp.zeros((NA, AUXB - QS), jnp.int32)], axis=1)
    tail = jnp.concatenate([tail, jnp.zeros((8 - NA, AUXB), jnp.int32)], axis=0)
    out[PART : PART + 8, :] = tail.astype(F32).astype(BF16)


def pack(aux_list, aux_count, metric):
    return pl.pallas_call(
        pack_kernel,
        out_shape=jax.ShapeDtypeStruct((PART + 8, AUXB), BF16),
        in_specs=[VMEM] * 3,
        out_specs=VMEM,
        compiler_params=PARAMS,
        name="pack",
    )(aux_list, aux_count, metric)


def line_kernel(sc_ref, m0, m1, m2, m3, out):
    zh = sc_ref[1]
    parts = [m[...].astype(F32) for m in (m0, m1, m2, m3)]
    rows = lax.broadcasted_iota(jnp.int32, (8, AUXB), 0)
    tail = jnp.zeros((8, AUXB), F32)
    for src in range(4):
        k = back(zh, src)
        near = jnp.where(k == 0, parts[0], parts[1])
        far = jnp.where(k == 2, parts[2], parts[3])
        part = jnp.where(k < 2, near, far)
        for q in range(QB):
            at = (4 * q + src) * MROWS
            out[at : at + MROWS, :] = part[q * MROWS : (q + 1) * MROWS, :].astype(BF16)
        for a in range(NA):
            tail = jnp.where(rows == NA * src + a, part[PART + a : PART + a + 1, :], tail)
    both = jnp.concatenate([tail, parts[0][PART : PART + 8, :]], axis=0)
    out[LIST0:SMALL, :] = both.astype(BF16)


def line(sc, parts):
    return pl.pallas_call(
        line_kernel,
        out_shape=jax.ShapeDtypeStruct((SMALL, AUXB), BF16),
        in_specs=[SMEM] + [VMEM] * 4,
        out_specs=VMEM,
        compiler_params=PARAMS,
        name="line",
    )(sc, *parts)


def fill(tiles, start, met, lists, row, dense, base):
    for i in range(QS):
        q = lists[row, i]
        at = start + i * BS
        fitted = jnp.dot(tiles[at : at + BS, :], met[q], preferred_element_type=F32)
        cols = pl.ds(pl.multiple_of(q * AUXB, AUXB), AUXB)
        dense[pl.ds(pl.multiple_of(base, BS), BS), cols] = fitted.astype(BF16)


def fill_block(tiles, met, lists, row, dense, base):
    for a in range(NA):
        fill(tiles, a * HALF, met, lists, row + a, dense, base + a * BS)


def read_lists(small):
    return small[LIST0:SMALL, :].astype(F32).astype(jnp.int32)


def build_kernel(sc_ref, t0, t1, t2, t3, z1, z3, f1, f3, s0, s1, s2, s3, dy, dz, met, lv, ls, sem):
    y, zh = sc_ref[0], sc_ref[1]
    for k, s in enumerate((s0, s1, s2, s3)):
        lv[16 * k : 16 * k + 16, :] = read_lists(s)
    copy = pltpu.make_async_copy(lv, ls, sem)
    copy.start()
    for k, s in enumerate((s0, s1, s2, s3)):
        at = pl.multiple_of(back(y, k) * 4 * MROWS, 4 * MROWS)
        met[0:QB, pl.ds(at, 4 * MROWS), :] = s[0:LIST0, :].reshape(QB, 4 * MROWS, AUXB)
    dy[...] = jnp.zeros_like(dy)
    dz[...] = jnp.zeros_like(dz)
    copy.wait()
    fill_block(t0, met, ls, 8, dy, y * ROWS)
    mine = dy[pl.ds(pl.multiple_of(y * ROWS, ROWS), ROWS), :]
    dz[pl.ds(pl.multiple_of(zh * ROWS, ROWS), ROWS), :] = mine
    for k, t in ((1, t1), (2, t2), (3, t3)):
        fill_block(t, met, ls, 16 * k + 8, dy, back(y, k) * ROWS)
    for k, t in ((1, z1), (3, z3)):
        src = back(zh, k)
        fill_block(t, met, ls, NA * src, dz, src * ROWS)
    src = back(zh, 2)
    for a, f in enumerate((f1, f3)):
        fill(f, 0, met, ls, NA * src + a, dz, src * ROWS + a * BS)


def build(sc, tiles, zs, smalls):
    dense = jax.ShapeDtypeStruct((4 * ROWS, WIDE), BF16)
    return pl.pallas_call(
        build_kernel,
        out_shape=(dense, dense),
        in_specs=[SMEM] + [VMEM] * 12,
        out_specs=(VMEM,) * 2,
        scratch_shapes=[
            pltpu.VMEM((QB + 1, AUXB, AUXB), BF16),
            pltpu.VMEM((64, 128), jnp.int32),
            pltpu.SMEM((64, 128), jnp.int32),
            pltpu.SemaphoreType.DMA,
        ],
        compiler_params=PARAMS,
        name="build",
    )(sc, *tiles, *zs, *smalls)


def gram_kernel(flip, picks, sc_ref, dy, dz, out):
    zh, co = sc_ref[1], sc_ref[2]
    parity = 1 - co if flip else co
    opposite = back(zh, 2)
    factor = 1.0 / (QS * 16 * AUXB) ** 0.5
    for slot, h in enumerate(picks):
        p = 2 * h + parity
        block = dz[pl.ds(pl.multiple_of(p * ROWS, ROWS), ROWS), 0:USED]

        def product(swapped, block=block, slot=slot):
            for q in range(4):
                row = dy[q * ROWS : (q + 1) * ROWS, 0:USED]
                pair = (block, row) if swapped else (row, block)
                prod = lax.dot_general(*pair, (((1,), (1,)), ((), ())), preferred_element_type=F32)
                out[q, slot] = prod * factor

        pl.when(p == opposite)(lambda: product(True))
        pl.when(p != opposite)(lambda: product(False))


def gram(flip, picks, sc, dy, dz):
    return pl.pallas_call(
        functools.partial(gram_kernel, flip, picks),
        out_shape=jax.ShapeDtypeStruct((4, len(picks), ROWS, ROWS), F32),
        in_specs=[SMEM] + [VMEM] * 2,
        out_specs=VMEM,
        compiler_params=PARAMS,
    )(sc, dy, dz)


def hold_kernel(tiles, late, out):
    out[...] = tiles[...]


def hold(tiles, late):
    return pl.pallas_call(
        hold_kernel,
        out_shape=jax.ShapeDtypeStruct(tiles.shape, tiles.dtype),
        in_specs=[VMEM] * 2,
        out_specs=VMEM,
        compiler_params=PARAMS,
        name="hold",
    )(tiles, late)


STEPS = tuple((k, w) for w in range(2) for k in range(4))


def share_kernel(sc_ref, keep, got0, got1, *outs):
    x, zl = sc_ref[3], sc_ref[4]

    def write(low):
        for (k, w), out in zip(STEPS, outs):
            q, h = lax.rem(x + k, 4), w if low else 1 - w
            got = got1 if h else got0
            out[...] = (keep[q, h] + got[q, 0]).astype(out.dtype)

    pl.when(zl == 0)(lambda: write(True))
    pl.when(zl != 0)(lambda: write(False))


def share(sc, keep, got0, got1):
    piece = (ROWS, ROWS)
    return pl.pallas_call(
        share_kernel,
        out_shape=(jax.ShapeDtypeStruct(piece, F32),) + (jax.ShapeDtypeStruct(piece, BF16),) * 7,
        in_specs=[SMEM] + [VMEM] * 3,
        out_specs=(VMEM,) * 8,
        compiler_params=PARAMS,
        name="share",
    )(sc, keep, got0, got1)


def hop(k, w):
    return [(2 * a + b, 2 * ((a + k) % 4) + (b + w) % 2) for a in range(4) for b in range(2)]


def homes():
    moves = []
    for n in range(256):
        y, z, x, p = n // 64, n // 16 % 4, n // 4 % 4, n % 4
        home = (x, z, y, p) if p == (z + 2) % 4 else (y, p, x, z)
        moves.append((n, home[0] * 64 + home[1] * 16 + home[2] * 4 + home[3]))
    return moves


def local(fit_tiles, aux_list, aux_count, metric):
    sc = jnp.stack([lax.axis_index(n) for n in ("y", "zh", "co", "x", "zl")]).astype(jnp.int32)
    part = pack(aux_list, aux_count, metric.reshape(PART, AUXB))
    parts = [part] + [lax.ppermute(part, "zh", ring(4, k)) for k in (1, 2, 3)]
    tiles = fit_tiles.reshape(2 * HALF, AUXB)
    z1 = lax.ppermute(tiles, "zh", ring(4, 1))
    z3 = lax.ppermute(tiles, "zh", ring(4, 3))
    ys = [tiles] + [lax.ppermute(tiles, "y", ring(4, k)) for k in (1, 2, 3)]
    small = line(sc, parts)
    smalls = [small] + [lax.ppermute(small, "y", ring(4, k)) for k in (1, 2, 3)]
    f1 = lax.ppermute(z1[:HALF], "zh", ring(4, 1))
    f3 = lax.ppermute(z3[HALF:], "zh", ring(4, 3))

    mine = hold(tiles, part)
    dy, dz = build(sc, [mine] + ys[1:], [z1, z3, f1, f3], smalls)
    got = []
    for h in range(2):
        send = gram(True, (h,), sc, dy, dz)
        got.append(lax.ppermute(send, "co", ring(2, 1)))
    keep = gram(False, (0, 1), sc, dy, dz)
    total, *shares = share(sc, keep, *got)
    for (k, w), piece in zip(STEPS[1:], shares):
        total = total + lax.ppermute(piece, ("x", "zl"), hop(k, w)).astype(F32)
    return lax.ppermute(total, ("y", "zh", "x", "zl", "co"), homes())


def solution(mesh):
    fine = Mesh(mesh.devices.reshape(4, 4, 4, 2, 2), ("y", "zh", "x", "zl", "co"))
    row, col = ("y", "zh"), ("x", "zl", "co")
    placed = (P(row, col, None, None), P(row, col), P(row, col), P(col, row, None))

    return jax.shard_map(local, mesh=fine, in_specs=placed, out_specs=P(col, row), check_vma=False)
```

profile of v0, /device:TPU:56, one launch (start us, length us, event | category | flops | bytes accessed | tf_op | source)
XLA Modules:
  0.0 113.6 jit_solution(677903269998263276)
XLA Ops:
  0.0 5.4 %collective-permute-start.4 = (bf16[1536,128]{1,0:T(8,128)(2,1)}, bf16[1536,128]{1,0:T(8,128)(2,1)S(1)}, u32[]{:S(2)}, u32[]{:S(2)}) collective-permute-start(bf16[1536,128]{1,0:T(8,128)(2,1)} %bitcast.7), channel_id=1, source_target_pairs={{0,48},{16,0},{32,16},{48,32},{1,49},{17,1},{33,17},{49,33},{2,50}... | collective-permute-start | bytes 1179656 | tf_op jit(solution)/shard_map/ppermute | solution.py:243
  5.4 0.7 copy.5.counts
  7.6 4.1 %collective-permute-start.9 = (bf16[104,128]{1,0:T(8,128)(2,1)S(1)}, bf16[104,128]{1,0:T(8,128)(2,1)S(1)}, u32[]{:S(2)}, u32[]{:S(2)}) collective-permute-start(bf16[104,128]{1,0:T(8,128)(2,1)S(1)} %pack.1.late.m0), channel_id=1, source_target_pairs={{0,48},{16,0},{32,16},{48,32},{1,49},{17,1},{33,17},{49,33},{2,50}... | collective-permute-start | bytes 79880 | tf_op jit(solution)/shard_map/ppermute | solution.py:240
  11.8 1.4 %collective-permute-start.8 = (bf16[104,128]{1,0:T(8,128)(2,1)S(1)}, bf16[104,128]{1,0:T(8,128)(2,1)S(1)}, u32[]{:S(2)}, u32[]{:S(2)}) collective-permute-start(bf16[104,128]{1,0:T(8,128)(2,1)S(1)} %pack.1.late.m0), channel_id=1, source_target_pairs={{0,32},{16,48},{32,0},{48,16},{1,33},{17,49},{33,1},{49,17},{2,34}... | collective-permute-start | bytes 79880 | tf_op jit(solution)/shard_map/ppermute | solution.py:240
  13.2 1.2 %collective-permute-start.7 = (bf16[104,128]{1,0:T(8,128)(2,1)S(1)}, bf16[104,128]{1,0:T(8,128)(2,1)S(1)}, u32[]{:S(2)}, u32[]{:S(2)}) collective-permute-start(bf16[104,128]{1,0:T(8,128)(2,1)S(1)} %pack.1.late.m0), channel_id=1, source_target_pairs={{0,16},{16,32},{32,48},{48,0},{1,17},{17,33},{33,49},{49,1},{2,18}... | collective-permute-start | bytes 79880 | tf_op jit(solution)/shard_map/ppermute | solution.py:240
  14.5 8.5 %collective-permute-done.9.m3 = bf16[104,128]{1,0:T(8,128)(2,1)S(1)} collective-permute-done((bf16[104,128]{1,0:T(8,128)(2,1)S(1)}, bf16[104,128]{1,0:T(8,128)(2,1)S(1)}, u32[]{:S(2)}, u32[]{:S(2)}) %collective-permute-start.9) | collective-permute-done | bytes 26656 | tf_op jit(solution)/shard_map/ppermute | solution.py:240
  23.3 5.5 %collective-permute-done.7.m1 = bf16[104,128]{1,0:T(8,128)(2,1)S(1)} collective-permute-done((bf16[104,128]{1,0:T(8,128)(2,1)S(1)}, bf16[104,128]{1,0:T(8,128)(2,1)S(1)}, u32[]{:S(2)}, u32[]{:S(2)}) %collective-permute-start.7) | collective-permute-done | bytes 26656 | tf_op jit(solution)/shard_map/ppermute | solution.py:240
  29.4 0.8 collective-permute-start.12
  30.7 3.5 %collective-permute-start.1 = (bf16[1536,128]{1,0:T(8,128)(2,1)}, bf16[1536,128]{1,0:T(8,128)(2,1)S(1)}, u32[]{:S(2)}, u32[]{:S(2)}) collective-permute-start(bf16[1536,128]{1,0:T(8,128)(2,1)} %bitcast.10), channel_id=1, source_target_pairs={{0,128},{64,192},{128,0},{192,64},{1,129},{65,193},{129,1},{193,65... | collective-permute-start | bytes 1179656 | tf_op jit(solution)/shard_map/ppermute | solution.py:244
  34.2 2.3 %collective-permute-done.12.s3 = bf16[400,128]{1,0:T(8,128)(2,1)S(1)} collective-permute-done((bf16[400,128]{1,0:T(8,128)(2,1)S(1)}, bf16[400,128]{1,0:T(8,128)(2,1)S(1)}, u32[]{:S(2)}, u32[]{:S(2)}) %collective-permute-start.12) | collective-permute-done | bytes 102432 | tf_op jit(solution)/shard_map/ppermute | solution.py:246
  36.4 1.6 %collective-permute-start.11 = (bf16[400,128]{1,0:T(8,128)(2,1)S(1)}, bf16[400,128]{1,0:T(8,128)(2,1)S(1)}, u32[]{:S(2)}, u32[]{:S(2)}) collective-permute-start(bf16[400,128]{1,0:T(8,128)(2,1)S(1)} %line.1.s0), channel_id=1, source_target_pairs={{0,128},{64,192},{128,0},{192,64},{1,129},{65,193},{129,1},{193,65... | collective-permute-start | bytes 307208 | tf_op jit(solution)/shard_map/ppermute | solution.py:246
  38.0 3.1 %collective-permute-start.10 = (bf16[400,128]{1,0:T(8,128)(2,1)S(1)}, bf16[400,128]{1,0:T(8,128)(2,1)S(1)}, u32[]{:S(2)}, u32[]{:S(2)}) collective-permute-start(bf16[400,128]{1,0:T(8,128)(2,1)S(1)} %line.1.s0), channel_id=1, source_target_pairs={{0,64},{64,128},{128,192},{192,0},{1,65},{65,129},{129,193},{193,1... | collective-permute-start | bytes 307208 | tf_op jit(solution)/shard_map/ppermute | solution.py:246
  41.2 12.1 %collective-permute-done.11.s2 = bf16[400,128]{1,0:T(8,128)(2,1)S(1)} collective-permute-done((bf16[400,128]{1,0:T(8,128)(2,1)S(1)}, bf16[400,128]{1,0:T(8,128)(2,1)S(1)}, u32[]{:S(2)}, u32[]{:S(2)}) %collective-permute-start.11) | collective-permute-done | bytes 102432 | tf_op jit(solution)/shard_map/ppermute | solution.py:246
  53.8 1.5 %collective-permute-done.10.s1 = bf16[400,128]{1,0:T(8,128)(2,1)S(1)} collective-permute-done((bf16[400,128]{1,0:T(8,128)(2,1)S(1)}, bf16[400,128]{1,0:T(8,128)(2,1)S(1)}, u32[]{:S(2)}, u32[]{:S(2)}) %collective-permute-start.10) | collective-permute-done | bytes 102432 | tf_op jit(solution)/shard_map/ppermute | solution.py:246
  55.3 0.9 collective-permute-start.5
  56.2 1.0 copy-done
  57.3 4.1 %collective-permute-done.6.f3 = bf16[768,128]{1,0:T(8,128)(2,1)S(1)} collective-permute-done((bf16[768,128]{1,0:T(8,128)(2,1)S(1)}, bf16[768,128]{1,0:T(8,128)(2,1)S(1)}, u32[]{:S(2)}, u32[]{:S(2)}) %collective-permute-start.6) | collective-permute-done | bytes 196640 | tf_op jit(solution)/shard_map/ppermute | solution.py:248
  61.4 4.2 %collective-permute-done.5.f1 = bf16[768,128]{1,0:T(8,128)(2,1)S(1)} collective-permute-done((bf16[768,128]{1,0:T(8,128)(2,1)S(1)}, bf16[768,128]{1,0:T(8,128)(2,1)S(1)}, u32[]{:S(2)}, u32[]{:S(2)}) %collective-permute-start.5) | collective-permute-done | bytes 196640 | tf_op jit(solution)/shard_map/ppermute | solution.py:247
  65.6 3.1 %build.1 = (bf16[1024,1664]{1,0:T(8,128)(2,1)S(1)}, bf16[1024,1664]{1,0:T(8,128)(2,1)S(1)}) custom-call(s32[5]{0:T(128)S(1)} %stack.23.sc_ref, bf16[1536,128]{1,0:T(8,128)(2,1)S(1)} %hold.1.t0, bf16[1536,128]{1,0:T(8,128)(2,1)S(1)} %collective-permute-done.t1, bf16[1536,128]{1,0:T(8,128)(2,1)S(1)} %collective-permute-done.1.t2, ...), custom_call_target="tpu_custom_call" | custom-call | tf_op jit(solution)/shard_map/build/pallas_call | solution.py:135
  68.7 1.8 %shard_map.48 = f32[4,1,256,256]{3,2,1,0:T(8,128)S(1)} custom-call(s32[5]{0:T(128)S(1)} %stack.23.sc_ref, bf16[1024,1664]{1,0:T(8,128)(2,1)S(1)} %get-tuple-element.15.dy, bf16[1024,1664]{1,0:T(8,128)(2,1)S(1)} %get-tuple-element.16.dz), custom_call_target="tpu_custom_call" | custom-call | tf_op jit(solution)/shard_map/pallas_call | solution.py:172
  70.5 1.6 %shard_map.47 = f32[4,1,256,256]{3,2,1,0:T(8,128)S(1)} custom-call(s32[5]{0:T(128)S(1)} %stack.23.sc_ref, bf16[1024,1664]{1,0:T(8,128)(2,1)S(1)} %get-tuple-element.15.dy, bf16[1024,1664]{1,0:T(8,128)(2,1)S(1)} %get-tuple-element.16.dz), custom_call_target="tpu_custom_call" | custom-call | tf_op jit(solution)/shard_map/pallas_call | solution.py:172
  72.8 2.7 %shard_map.46.keep = f32[4,2,256,256]{3,2,1,0:T(8,128)S(1)} custom-call(s32[5]{0:T(128)S(1)} %stack.23.sc_ref, bf16[1024,1664]{1,0:T(8,128)(2,1)S(1)} %get-tuple-element.15.dy, bf16[1024,1664]{1,0:T(8,128)(2,1)S(1)} %get-tuple-element.16.dz), custom_call_target="tpu_custom_call" | custom-call | tf_op jit(solution)/shard_map/pallas_call | solution.py:172
  75.5 0.9 collective-permute-done.14.got1
  77.2 1.6 %collective-permute-start.15 = (bf16[256,256]{1,0:T(8,128)(2,1)S(1)}, bf16[256,256]{1,0:T(8,128)(2,1)S(1)}, u32[]{:S(2)}, u32[]{:S(2)}) collective-permute-start(bf16[256,256]{1,0:T(8,128)(2,1)S(1)} %get-tuple-element.18), channel_id=1, source_target_pairs={{0,4},{2,6},{4,8},{6,10},{8,12},{10,14},{12,0},{14,2},{1,5},{3,7},... | collective-permute-start | bytes 393224 | tf_op jit(solution)/shard_map/ppermute | solution.py:259
  78.7 2.7 %collective-permute-start.16 = (bf16[256,256]{1,0:T(8,128)(2,1)S(1)}, bf16[256,256]{1,0:T(8,128)(2,1)S(1)}, u32[]{:S(2)}, u32[]{:S(2)}) collective-permute-start(bf16[256,256]{1,0:T(8,128)(2,1)S(1)} %get-tuple-element.19), channel_id=1, source_target_pairs={{0,8},{2,10},{4,12},{6,14},{8,0},{10,2},{12,4},{14,6},{1,9},{3,11}... | collective-permute-start | bytes 393224 | tf_op jit(solution)/shard_map/ppermute | solution.py:259
  81.5 1.4 %collective-permute-start.17 = (bf16[256,256]{1,0:T(8,128)(2,1)S(1)}, bf16[256,256]{1,0:T(8,128)(2,1)S(1)}, u32[]{:S(2)}, u32[]{:S(2)}) collective-permute-start(bf16[256,256]{1,0:T(8,128)(2,1)S(1)} %get-tuple-element.20), channel_id=1, source_target_pairs={{0,12},{2,14},{4,0},{6,2},{8,4},{10,6},{12,8},{14,10},{1,13},{3,15... | collective-permute-start | bytes 393224 | tf_op jit(solution)/shard_map/ppermute | solution.py:259
  82.9 2.0 %collective-permute-start.19 = (bf16[256,256]{1,0:T(8,128)(2,1)S(1)}, bf16[256,256]{1,0:T(8,128)(2,1)S(1)}, u32[]{:S(2)}, u32[]{:S(2)}) collective-permute-start(bf16[256,256]{1,0:T(8,128)(2,1)S(1)} %get-tuple-element.22), channel_id=1, source_target_pairs={{0,6},{2,4},{4,10},{6,8},{8,14},{10,12},{12,2},{14,0},{1,7},{3,5},... | collective-permute-start | bytes 393224 | tf_op jit(solution)/shard_map/ppermute | solution.py:259
  85.3 7.2 %collective-permute-done.16 = bf16[256,256]{1,0:T(8,128)(2,1)S(1)} collective-permute-done((bf16[256,256]{1,0:T(8,128)(2,1)S(1)}, bf16[256,256]{1,0:T(8,128)(2,1)S(1)}, u32[]{:S(2)}, u32[]{:S(2)}) %collective-permute-start.16) | collective-permute-done | bytes 131104 | tf_op jit(solution)/shard_map/ppermute | solution.py:259
  92.5 2.0 %collective-permute-done.20 = bf16[256,256]{1,0:T(8,128)(2,1)S(1)} collective-permute-done((bf16[256,256]{1,0:T(8,128)(2,1)S(1)}, bf16[256,256]{1,0:T(8,128)(2,1)S(1)}, u32[]{:S(2)}, u32[]{:S(2)}) %collective-permute-start.20) | collective-permute-done | bytes 131104 | tf_op jit(solution)/shard_map/ppermute | solution.py:259
  94.6 3.8 %collective-permute-done.21 = bf16[256,256]{1,0:T(8,128)(2,1)S(1)} collective-permute-done((bf16[256,256]{1,0:T(8,128)(2,1)S(1)}, bf16[256,256]{1,0:T(8,128)(2,1)S(1)}, u32[]{:S(2)}, u32[]{:S(2)}) %collective-permute-start.21) | collective-permute-done | bytes 131104 | tf_op jit(solution)/shard_map/ppermute | solution.py:259
  98.5 5.0 %collective-permute-start.22 = (f32[256,256]{1,0:T(8,128)S(1)}, f32[256,256]{1,0:T(8,128)S(1)}, u32[]{:S(2)}, u32[]{:S(2)}) collective-permute-start(f32[256,256]{1,0:T(8,128)S(1)} %convert_add_fusion), channel_id=1, source_target_pairs={{0,0},{1,16},{2,2},{3,48},{4,4},{5,20},{6,66},{7,52},{8,8},{9,24},... | collective-permute-start | bytes 786440 | tf_op jit(solution)/shard_map/ppermute | solution.py:260
  103.6 9.4 %collective-permute-done.22 = f32[256,256]{1,0:T(8,128)S(1)} collective-permute-done((f32[256,256]{1,0:T(8,128)S(1)}, f32[256,256]{1,0:T(8,128)S(1)}, u32[]{:S(2)}, u32[]{:S(2)}) %collective-permute-start.22) | collective-permute-done | bytes 262176 | tf_op jit(solution)/shard_map/ppermute | solution.py:260
  (34 shorter events, 6.0 us)
Async XLA Ops:
  0.0 36.4 %collective-permute-start.4 = (bf16[1536,128]{1,0:T(8,128)(2,1)}, bf16[1536,128]{1,0:T(8,128)(2,1)S(1)}, u32[]{:S(2)}, u32[]{:S(2)}) collective-permute-start(bf16[1536,128]{1,0:T(8,128)(2,1)} %bitcast.7), channel_id=1, source_target_pairs={{0,48},{16,0},{32,16},{48,32},{1,49},{17,1},{33,17},{49,33},{2,50}... | collective-permute-start | bytes 1179656 | tf_op jit(solution)/shard_map/ppermute | solution.py:243
  5.4 32.6 %collective-permute-start.3 = (bf16[1536,128]{1,0:T(8,128)(2,1)}, bf16[1536,128]{1,0:T(8,128)(2,1)S(1)}, u32[]{:S(2)}, u32[]{:S(2)}) collective-permute-start(bf16[1536,128]{1,0:T(8,128)(2,1)} %bitcast.8), channel_id=1, source_target_pairs={{0,16},{16,32},{32,48},{48,0},{1,17},{17,33},{33,49},{49,1},{2,18}... | collective-permute-start | bytes 1179656 | tf_op jit(solution)/shard_map/ppermute | solution.py:242
  6.1 0.7 copy-start.1
  6.9 0.7 copy-start.2
  7.6 15.4 %collective-permute-start.9 = (bf16[104,128]{1,0:T(8,128)(2,1)S(1)}, bf16[104,128]{1,0:T(8,128)(2,1)S(1)}, u32[]{:S(2)}, u32[]{:S(2)}) collective-permute-start(bf16[104,128]{1,0:T(8,128)(2,1)S(1)} %pack.1.late.m0), channel_id=1, source_target_pairs={{0,48},{16,0},{32,16},{48,32},{1,49},{17,1},{33,17},{49,33},{2,50}... | collective-permute-start | bytes 79880 | tf_op jit(solution)/shard_map/ppermute | solution.py:240
  11.8 11.5 %collective-permute-start.8 = (bf16[104,128]{1,0:T(8,128)(2,1)S(1)}, bf16[104,128]{1,0:T(8,128)(2,1)S(1)}, u32[]{:S(2)}, u32[]{:S(2)}) collective-permute-start(bf16[104,128]{1,0:T(8,128)(2,1)S(1)} %pack.1.late.m0), channel_id=1, source_target_pairs={{0,32},{16,48},{32,0},{48,16},{1,33},{17,49},{33,1},{49,17},{2,34}... | collective-permute-start | bytes 79880 | tf_op jit(solution)/shard_map/ppermute | solution.py:240
  13.2 15.6 %collective-permute-start.7 = (bf16[104,128]{1,0:T(8,128)(2,1)S(1)}, bf16[104,128]{1,0:T(8,128)(2,1)S(1)}, u32[]{:S(2)}, u32[]{:S(2)}) collective-permute-start(bf16[104,128]{1,0:T(8,128)(2,1)S(1)} %pack.1.late.m0), channel_id=1, source_target_pairs={{0,16},{16,32},{32,48},{48,0},{1,17},{17,33},{33,49},{49,1},{2,18}... | collective-permute-start | bytes 79880 | tf_op jit(solution)/shard_map/ppermute | solution.py:240
  29.4 7.0 %collective-permute-start.12 = (bf16[400,128]{1,0:T(8,128)(2,1)S(1)}, bf16[400,128]{1,0:T(8,128)(2,1)S(1)}, u32[]{:S(2)}, u32[]{:S(2)}) collective-permute-start(bf16[400,128]{1,0:T(8,128)(2,1)S(1)} %line.1.s0), channel_id=1, source_target_pairs={{0,192},{64,0},{128,64},{192,128},{1,193},{65,1},{129,65},{193,129... | collective-permute-start | bytes 307208 | tf_op jit(solution)/shard_map/ppermute | solution.py:246
  30.2 27.0 %collective-permute-start.2 = (bf16[1536,128]{1,0:T(8,128)(2,1)}, bf16[1536,128]{1,0:T(8,128)(2,1)S(1)}, u32[]{:S(2)}, u32[]{:S(2)}) collective-permute-start(bf16[1536,128]{1,0:T(8,128)(2,1)} %bitcast.9), channel_id=1, source_target_pairs={{0,192},{64,0},{128,64},{192,128},{1,193},{65,1},{129,65},{193,129... | collective-permute-start | bytes 1179656 | tf_op jit(solution)/shard_map/ppermute | solution.py:244
  30.7 26.6 %collective-permute-start.1 = (bf16[1536,128]{1,0:T(8,128)(2,1)}, bf16[1536,128]{1,0:T(8,128)(2,1)S(1)}, u32[]{:S(2)}, u32[]{:S(2)}) collective-permute-start(bf16[1536,128]{1,0:T(8,128)(2,1)} %bitcast.10), channel_id=1, source_target_pairs={{0,128},{64,192},{128,0},{192,64},{1,129},{65,193},{129,1},{193,65... | collective-permute-start | bytes 1179656 | tf_op jit(solution)/shard_map/ppermute | solution.py:244
  36.4 20.8 %collective-permute-start = (bf16[1536,128]{1,0:T(8,128)(2,1)}, bf16[1536,128]{1,0:T(8,128)(2,1)S(1)}, u32[]{:S(2)}, u32[]{:S(2)}) collective-permute-start(bf16[1536,128]{1,0:T(8,128)(2,1)} %bitcast.11), channel_id=1, source_target_pairs={{0,64},{64,128},{128,192},{192,0},{1,65},{65,129},{129,193},{193,1... | collective-permute-start | bytes 1179656 | tf_op jit(solution)/shard_map/ppermute | solution.py:244
  36.4 16.9 %collective-permute-start.11 = (bf16[400,128]{1,0:T(8,128)(2,1)S(1)}, bf16[400,128]{1,0:T(8,128)(2,1)S(1)}, u32[]{:S(2)}, u32[]{:S(2)}) collective-permute-start(bf16[400,128]{1,0:T(8,128)(2,1)S(1)} %line.1.s0), channel_id=1, source_target_pairs={{0,128},{64,192},{128,0},{192,64},{1,129},{65,193},{129,1},{193,65... | collective-permute-start | bytes 307208 | tf_op jit(solution)/shard_map/ppermute | solution.py:246
  38.0 17.3 %collective-permute-start.10 = (bf16[400,128]{1,0:T(8,128)(2,1)S(1)}, bf16[400,128]{1,0:T(8,128)(2,1)S(1)}, u32[]{:S(2)}, u32[]{:S(2)}) collective-permute-start(bf16[400,128]{1,0:T(8,128)(2,1)S(1)} %line.1.s0), channel_id=1, source_target_pairs={{0,64},{64,128},{128,192},{192,0},{1,65},{65,129},{129,193},{193,1... | collective-permute-start | bytes 307208 | tf_op jit(solution)/shard_map/ppermute | solution.py:246
  53.3 8.1 %collective-permute-start.6 = (bf16[768,128]{1,0:T(8,128)(2,1)S(1)}, bf16[768,128]{1,0:T(8,128)(2,1)S(1)}, u32[]{:S(2)}, u32[]{:S(2)}) collective-permute-start(bf16[768,128]{1,0:T(8,128)(2,1)S(1)} %slice.9), channel_id=1, source_target_pairs={{0,48},{16,0},{32,16},{48,32},{1,49},{17,1},{33,17},{49,33},{2,50}... | collective-permute-start | bytes 589832 | tf_op jit(solution)/shard_map/ppermute | solution.py:248
  55.3 10.3 %collective-permute-start.5 = (bf16[768,128]{1,0:T(8,128)(2,1)S(1)}, bf16[768,128]{1,0:T(8,128)(2,1)S(1)}, u32[]{:S(2)}, u32[]{:S(2)}) collective-permute-start(bf16[768,128]{1,0:T(8,128)(2,1)S(1)} %slice.8), channel_id=1, source_target_pairs={{0,16},{16,32},{32,48},{48,0},{1,17},{17,33},{33,49},{49,1},{2,18}... | collective-permute-start | bytes 589832 | tf_op jit(solution)/shard_map/ppermute | solution.py:247
  56.2 1.0 copy-start
  72.2 3.3 %collective-permute-start.13 = (f32[4,1,256,256]{3,2,1,0:T(8,128)S(1)}, f32[4,1,256,256]{3,2,1,0:T(8,128)S(1)}, u32[]{:S(2)}, u32[]{:S(2)}) collective-permute-start(f32[4,1,256,256]{3,2,1,0:T(8,128)S(1)} %shard_map.47), channel_id=1, source_target_pairs={{0,1},{1,0},{2,3},{3,2},{4,5},{5,4},{6,7},{7,6},{8,9},{9,8},{10,11... | collective-permute-start | bytes 3145736 | tf_op jit(solution)/shard_map/ppermute | solution.py:255
  72.3 4.1 %collective-permute-start.14 = (f32[4,1,256,256]{3,2,1,0:T(8,128)S(1)}, f32[4,1,256,256]{3,2,1,0:T(8,128)S(1)}, u32[]{:S(2)}, u32[]{:S(2)}) collective-permute-start(f32[4,1,256,256]{3,2,1,0:T(8,128)S(1)} %shard_map.48), channel_id=1, source_target_pairs={{0,1},{1,0},{2,3},{3,2},{4,5},{5,4},{6,7},{7,6},{8,9},{9,8},{10,11... | collective-permute-start | bytes 3145736 | tf_op jit(solution)/shard_map/ppermute | solution.py:255
  77.2 7.8 %collective-permute-start.15 = (bf16[256,256]{1,0:T(8,128)(2,1)S(1)}, bf16[256,256]{1,0:T(8,128)(2,1)S(1)}, u32[]{:S(2)}, u32[]{:S(2)}) collective-permute-start(bf16[256,256]{1,0:T(8,128)(2,1)S(1)} %get-tuple-element.18), channel_id=1, source_target_pairs={{0,4},{2,6},{4,8},{6,10},{8,12},{10,14},{12,0},{14,2},{1,5},{3,7},... | collective-permute-start | bytes 393224 | tf_op jit(solution)/shard_map/ppermute | solution.py:259
  78.7 13.8 %collective-permute-start.16 = (bf16[256,256]{1,0:T(8,128)(2,1)S(1)}, bf16[256,256]{1,0:T(8,128)(2,1)S(1)}, u32[]{:S(2)}, u32[]{:S(2)}) collective-permute-start(bf16[256,256]{1,0:T(8,128)(2,1)S(1)} %get-tuple-element.19), channel_id=1, source_target_pairs={{0,8},{2,10},{4,12},{6,14},{8,0},{10,2},{12,4},{14,6},{1,9},{3,11}... | collective-permute-start | bytes 393224 | tf_op jit(solution)/shard_map/ppermute | solution.py:259
  81.5 11.1 %collective-permute-start.17 = (bf16[256,256]{1,0:T(8,128)(2,1)S(1)}, bf16[256,256]{1,0:T(8,128)(2,1)S(1)}, u32[]{:S(2)}, u32[]{:S(2)}) collective-permute-start(bf16[256,256]{1,0:T(8,128)(2,1)S(1)} %get-tuple-element.20), channel_id=1, source_target_pairs={{0,12},{2,14},{4,0},{6,2},{8,4},{10,6},{12,8},{14,10},{1,13},{3,15... | collective-permute-start | bytes 393224 | tf_op jit(solution)/shard_map/ppermute | solution.py:259
  82.9 9.6 %collective-permute-start.18 = (bf16[256,256]{1,0:T(8,128)(2,1)S(1)}, bf16[256,256]{1,0:T(8,128)(2,1)S(1)}, u32[]{:S(2)}, u32[]{:S(2)}) collective-permute-start(bf16[256,256]{1,0:T(8,128)(2,1)S(1)} %get-tuple-element.21), channel_id=1, source_target_pairs={{0,2},{2,0},{4,6},{6,4},{8,10},{10,8},{12,14},{14,12},{1,3},{3,1},... | collective-permute-start | bytes 393224 | tf_op jit(solution)/shard_map/ppermute | solution.py:259
  82.9 9.6 %collective-permute-start.19 = (bf16[256,256]{1,0:T(8,128)(2,1)S(1)}, bf16[256,256]{1,0:T(8,128)(2,1)S(1)}, u32[]{:S(2)}, u32[]{:S(2)}) collective-permute-start(bf16[256,256]{1,0:T(8,128)(2,1)S(1)} %get-tuple-element.22), channel_id=1, source_target_pairs={{0,6},{2,4},{4,10},{6,8},{8,14},{10,12},{12,2},{14,0},{1,7},{3,5},... | collective-permute-start | bytes 393224 | tf_op jit(solution)/shard_map/ppermute | solution.py:259
  85.0 9.6 %collective-permute-start.20 = (bf16[256,256]{1,0:T(8,128)(2,1)S(1)}, bf16[256,256]{1,0:T(8,128)(2,1)S(1)}, u32[]{:S(2)}, u32[]{:S(2)}) collective-permute-start(bf16[256,256]{1,0:T(8,128)(2,1)S(1)} %get-tuple-element.23), channel_id=1, source_target_pairs={{0,10},{2,8},{4,14},{6,12},{8,2},{10,0},{12,6},{14,4},{1,11},{3,9}... | collective-permute-start | bytes 393224 | tf_op jit(solution)/shard_map/ppermute | solution.py:259
  92.5 5.9 %collective-permute-start.21 = (bf16[256,256]{1,0:T(8,128)(2,1)S(1)}, bf16[256,256]{1,0:T(8,128)(2,1)S(1)}, u32[]{:S(2)}, u32[]{:S(2)}) collective-permute-start(bf16[256,256]{1,0:T(8,128)(2,1)S(1)} %get-tuple-element.24), channel_id=1, source_target_pairs={{0,14},{2,12},{4,2},{6,0},{8,6},{10,4},{12,10},{14,8},{1,15},{3,13... | collective-permute-start | bytes 393224 | tf_op jit(solution)/shard_map/ppermute | solution.py:259
  98.5 14.4 %collective-permute-start.22 = (f32[256,256]{1,0:T(8,128)S(1)}, f32[256,256]{1,0:T(8,128)S(1)}, u32[]{:S(2)}, u32[]{:S(2)}) collective-permute-start(f32[256,256]{1,0:T(8,128)S(1)} %convert_add_fusion), channel_id=1, source_target_pairs={{0,0},{1,16},{2,2},{3,48},{4,4},{5,20},{6,66},{7,52},{8,8},{9,24},... | collective-permute-start | bytes 786440 | tf_op jit(solution)/shard_map/ppermute | solution.py:260
where the time goes:
time: 114 us
  waiting for transfers between devices  61.9 us (54%)
  starting transfers between devices  36.8 us (32%)
  Pallas kernels  10.7 us (9%)
  local copies, waits for them, and re-layouts  3.97 us (3%)
    ppermute x3, waiting for transfers between devices, local(): smalls = [small] + [lax.ppermute(small, 'y', ring(4, k)) for k in (1, 2, 3)]  15.9 us
    ppermute x3, waiting for transfers between devices, local(): parts = [part] + [lax.ppermute(part, 'zh', ring(4, k)) for k in (1, 2, 3)]  14.3 us
    ppermute x7, waiting for transfers between devices, local(): total = total + lax.ppermute(piece, ('x', 'zl'), hop(k, w)).astype(F32)  13.1 us
    ppermute x1, waiting for transfers between devices, local(): return lax.ppermute(total, ('y', 'zh', 'x', 'zl', 'co'), homes())  9.36 us
    ppermute x7, starting transfers between devices, local(): total = total + lax.ppermute(piece, ('x', 'zl'), hop(k, w)).astype(F32)  8.1 us
    ppermute x3, starting transfers between devices, local(): parts = [part] + [lax.ppermute(part, 'zh', ring(4, k)) for k in (1, 2, 3)]  6.75 us
    pallas_call x3, Pallas kernels, gram(): pl.pallas_call(functools.partial(gram_kernel, flip, picks), out_shape=jax...  6.12 us
    ppermute x3, starting transfers between devices, local(): smalls = [small] + [lax.ppermute(small, 'y', ring(4, k)) for k in (1, 2, 3)]  5.52 us
  transfers between devices with their start and end apart: 23, of which 13 were waited for; matrix products, arithmetic and copies ran while one was open for 1% of the time, Pallas kernels for 3%

commit v1 on v0

--- a/solution.py
+++ b/solution.py
@@ -193,14 +193,15 @@
     )(tiles, late)
 
 
-STEPS = tuple((k, w) for w in range(2) for k in range(4))
-
-
-def share_kernel(sc_ref, keep, got0, got1, *outs):
+FIRST = ((2, 1), (2, 0))
+REST = ((1, 1), (3, 1), (1, 0), (3, 0), (0, 1), (0, 0))
+
+
+def share_kernel(steps, sc_ref, keep, got0, got1, *outs):
     x, zl = sc_ref[3], sc_ref[4]
 
     def write(low):
-        for (k, w), out in zip(STEPS, outs):
+        for (k, w), out in zip(steps, outs):
             q, h = lax.rem(x + k, 4), w if low else 1 - w
             got = got1 if h else got0
             out[...] = (keep[q, h] + got[q, 0]).astype(out.dtype)
@@ -209,13 +210,13 @@
     pl.when(zl != 0)(lambda: write(False))
 
 
-def share(sc, keep, got0, got1):
-    piece = (ROWS, ROWS)
-    return pl.pallas_call(
-        share_kernel,
-        out_shape=(jax.ShapeDtypeStruct(piece, F32),) + (jax.ShapeDtypeStruct(piece, BF16),) * 7,
+def share(steps, sc, keep, got0, got1):
+    kinds = [F32 if step == (0, 0) else BF16 for step in steps]
+    return pl.pallas_call(
+        functools.partial(share_kernel, steps),
+        out_shape=tuple(jax.ShapeDtypeStruct((ROWS, ROWS), kind) for kind in kinds),
         in_specs=[SMEM] + [VMEM] * 3,
-        out_specs=(VMEM,) * 8,
+        out_specs=(VMEM,) * len(steps),
         compiler_params=PARAMS,
         name="share",
     )(sc, keep, got0, got1)
@@ -254,8 +255,10 @@
         send = gram(True, (h,), sc, dy, dz)
         got.append(lax.ppermute(send, "co", ring(2, 1)))
     keep = gram(False, (0, 1), sc, dy, dz)
-    total, *shares = share(sc, keep, *got)
-    for (k, w), piece in zip(STEPS[1:], shares):
+    pieces = list(share(FIRST, sc, keep, *got))
+    pieces += share(REST, sc, keep, *got)
+    total = pieces.pop()
+    for (k, w), piece in zip(FIRST + REST, pieces):
         total = total + lax.ppermute(piece, ("x", "zl"), hop(k, w)).astype(F32)
     return lax.ppermute(total, ("y", "zh", "x", "zl", "co"), homes())
 

time: 114 us -> 112 us (0.982)
  the two profiles are of different devices: /device:TPU:56 before, /device:TPU:36 now
where the time goes in v1:
time: 112 us
  waiting for transfers between devices  62.8 us (56%)
  starting transfers between devices  33.6 us (30%)
  Pallas kernels  11.2 us (10%)
  local copies, waits for them, and re-layouts  3.97 us (4%)
    ppermute x3, waiting for transfers between devices, local(): smalls = [small] + [lax.ppermute(small, 'y', ring(4, k)) for k in (1, 2, 3)]  18.4 us
    ppermute x3, waiting for transfers between devices, local(): parts = [part] + [lax.ppermute(part, 'zh', ring(4, k)) for k in (1, 2, 3)]  14.3 us
    ppermute x7, waiting for transfers between devices, local(): total = total + lax.ppermute(piece, ('x', 'zl'), hop(k, w)).astype(F32)  11.2 us
    ppermute x1, waiting for transfers between devices, local(): return lax.ppermute(total, ('y', 'zh', 'x', 'zl', 'co'), homes())  9.88 us
    ppermute x3, starting transfers between devices, local(): smalls = [small] + [lax.ppermute(small, 'y', ring(4, k)) for k in (1, 2, 3)]  7.2 us
    ppermute x3, starting transfers between devices, local(): parts = [part] + [lax.ppermute(part, 'zh', ring(4, k)) for k in (1, 2, 3)]  6.75 us
    ppermute x7, starting transfers between devices, local(): total = total + lax.ppermute(piece, ('x', 'zl'), hop(k, w)).astype(F32)  6.71 us
    pallas_call x3, Pallas kernels, gram(): pl.pallas_call(functools.partial(gram_kernel, flip, picks), out_shape=jax...  6.13 us
  transfers between devices with their start and end apart: 23, of which 14 were waited for; matrix products, arithmetic and copies ran while one was open for 1% of the time, Pallas kernels for 4%

profile of v1, /device:TPU:36, one launch (start us, length us, event | category | flops | bytes accessed | tf_op | source)
XLA Modules:
  0.0 111.8 jit_solution(5582914745361787468)
XLA Ops:
  0.0 5.4 %collective-permute-start.4 = (bf16[1536,128]{1,0:T(8,128)(2,1)}, bf16[1536,128]{1,0:T(8,128)(2,1)S(1)}, u32[]{:S(2)}, u32[]{:S(2)}) collective-permute-start(bf16[1536,128]{1,0:T(8,128)(2,1)} %bitcast.7), channel_id=1, source_target_pairs={{0,48},{16,0},{32,16},{48,32},{1,49},{17,1},{33,17},{49,33},{2,50}... | collective-permute-start | bytes 1179656 | tf_op jit(solution)/shard_map/ppermute | solution.py:244
  5.4 0.7 copy.5.counts
  6.1 0.7 copy-done.1
  7.6 4.1 %collective-permute-start.9 = (bf16[104,128]{1,0:T(8,128)(2,1)S(1)}, bf16[104,128]{1,0:T(8,128)(2,1)S(1)}, u32[]{:S(2)}, u32[]{:S(2)}) collective-permute-start(bf16[104,128]{1,0:T(8,128)(2,1)S(1)} %pack.1.late.m0), channel_id=1, source_target_pairs={{0,48},{16,0},{32,16},{48,32},{1,49},{17,1},{33,17},{49,33},{2,50}... | collective-permute-start | bytes 79880 | tf_op jit(solution)/shard_map/ppermute | solution.py:241
  11.8 1.4 %collective-permute-start.8 = (bf16[104,128]{1,0:T(8,128)(2,1)S(1)}, bf16[104,128]{1,0:T(8,128)(2,1)S(1)}, u32[]{:S(2)}, u32[]{:S(2)}) collective-permute-start(bf16[104,128]{1,0:T(8,128)(2,1)S(1)} %pack.1.late.m0), channel_id=1, source_target_pairs={{0,32},{16,48},{32,0},{48,16},{1,33},{17,49},{33,1},{49,17},{2,34}... | collective-permute-start | bytes 79880 | tf_op jit(solution)/shard_map/ppermute | solution.py:241
  13.2 1.2 %collective-permute-start.7 = (bf16[104,128]{1,0:T(8,128)(2,1)S(1)}, bf16[104,128]{1,0:T(8,128)(2,1)S(1)}, u32[]{:S(2)}, u32[]{:S(2)}) collective-permute-start(bf16[104,128]{1,0:T(8,128)(2,1)S(1)} %pack.1.late.m0), channel_id=1, source_target_pairs={{0,16},{16,32},{32,48},{48,0},{1,17},{17,33},{33,49},{49,1},{2,18}... | collective-permute-start | bytes 79880 | tf_op jit(solution)/shard_map/ppermute | solution.py:241
  14.5 8.5 %collective-permute-done.9.m3 = bf16[104,128]{1,0:T(8,128)(2,1)S(1)} collective-permute-done((bf16[104,128]{1,0:T(8,128)(2,1)S(1)}, bf16[104,128]{1,0:T(8,128)(2,1)S(1)}, u32[]{:S(2)}, u32[]{:S(2)}) %collective-permute-start.9) | collective-permute-done | bytes 26656 | tf_op jit(solution)/shard_map/ppermute | solution.py:241
  23.3 5.5 %collective-permute-done.7.m1 = bf16[104,128]{1,0:T(8,128)(2,1)S(1)} collective-permute-done((bf16[104,128]{1,0:T(8,128)(2,1)S(1)}, bf16[104,128]{1,0:T(8,128)(2,1)S(1)}, u32[]{:S(2)}, u32[]{:S(2)}) %collective-permute-start.7) | collective-permute-done | bytes 26656 | tf_op jit(solution)/shard_map/ppermute | solution.py:241
  29.4 3.1 %collective-permute-start.12 = (bf16[400,128]{1,0:T(8,128)(2,1)S(1)}, bf16[400,128]{1,0:T(8,128)(2,1)S(1)}, u32[]{:S(2)}, u32[]{:S(2)}) collective-permute-start(bf16[400,128]{1,0:T(8,128)(2,1)S(1)} %line.1.s0), channel_id=1, source_target_pairs={{0,192},{64,0},{128,64},{192,128},{1,193},{65,1},{129,65},{193,129... | collective-permute-start | bytes 307208 | tf_op jit(solution)/shard_map/ppermute | solution.py:247
  32.5 0.7 collective-permute-start.2
  33.6 2.2 %collective-permute-done.12.s3 = bf16[400,128]{1,0:T(8,128)(2,1)S(1)} collective-permute-done((bf16[400,128]{1,0:T(8,128)(2,1)S(1)}, bf16[400,128]{1,0:T(8,128)(2,1)S(1)}, u32[]{:S(2)}, u32[]{:S(2)}) %collective-permute-start.12) | collective-permute-done | bytes 102432 | tf_op jit(solution)/shard_map/ppermute | solution.py:247
  35.8 1.0 collective-permute-start
  36.8 4.1 %collective-permute-start.11 = (bf16[400,128]{1,0:T(8,128)(2,1)S(1)}, bf16[400,128]{1,0:T(8,128)(2,1)S(1)}, u32[]{:S(2)}, u32[]{:S(2)}) collective-permute-start(bf16[400,128]{1,0:T(8,128)(2,1)S(1)} %line.1.s0), channel_id=1, source_target_pairs={{0,128},{64,192},{128,0},{192,64},{1,129},{65,193},{129,1},{193,65... | collective-permute-start | bytes 307208 | tf_op jit(solution)/shard_map/ppermute | solution.py:247
  41.0 15.8 %collective-permute-done.11.s2 = bf16[400,128]{1,0:T(8,128)(2,1)S(1)} collective-permute-done((bf16[400,128]{1,0:T(8,128)(2,1)S(1)}, bf16[400,128]{1,0:T(8,128)(2,1)S(1)}, u32[]{:S(2)}, u32[]{:S(2)}) %collective-permute-start.11) | collective-permute-done | bytes 102432 | tf_op jit(solution)/shard_map/ppermute | solution.py:247
  57.7 2.0 %collective-permute-start.5 = (bf16[768,128]{1,0:T(8,128)(2,1)S(1)}, bf16[768,128]{1,0:T(8,128)(2,1)S(1)}, u32[]{:S(2)}, u32[]{:S(2)}) collective-permute-start(bf16[768,128]{1,0:T(8,128)(2,1)S(1)} %slice.8), channel_id=1, source_target_pairs={{0,16},{16,32},{32,48},{48,0},{1,17},{17,33},{33,49},{49,1},{2,18}... | collective-permute-start | bytes 589832 | tf_op jit(solution)/shard_map/ppermute | solution.py:248
  59.7 1.0 copy-done
  60.7 3.4 %collective-permute-done.6.f3 = bf16[768,128]{1,0:T(8,128)(2,1)S(1)} collective-permute-done((bf16[768,128]{1,0:T(8,128)(2,1)S(1)}, bf16[768,128]{1,0:T(8,128)(2,1)S(1)}, u32[]{:S(2)}, u32[]{:S(2)}) %collective-permute-start.6) | collective-permute-done | bytes 196640 | tf_op jit(solution)/shard_map/ppermute | solution.py:249
  64.2 4.6 %collective-permute-done.5.f1 = bf16[768,128]{1,0:T(8,128)(2,1)S(1)} collective-permute-done((bf16[768,128]{1,0:T(8,128)(2,1)S(1)}, bf16[768,128]{1,0:T(8,128)(2,1)S(1)}, u32[]{:S(2)}, u32[]{:S(2)}) %collective-permute-start.5) | collective-permute-done | bytes 196640 | tf_op jit(solution)/shard_map/ppermute | solution.py:248
  68.7 3.1 %build.1 = (bf16[1024,1664]{1,0:T(8,128)(2,1)S(1)}, bf16[1024,1664]{1,0:T(8,128)(2,1)S(1)}) custom-call(s32[5]{0:T(128)S(1)} %stack.23.sc_ref, bf16[1536,128]{1,0:T(8,128)(2,1)S(1)} %hold.1.t0, bf16[1536,128]{1,0:T(8,128)(2,1)S(1)} %collective-permute-done.t1, bf16[1536,128]{1,0:T(8,128)(2,1)S(1)} %collective-permute-done.1.t2, ...), custom_call_target="tpu_custom_call" | custom-call | tf_op jit(solution)/shard_map/build/pallas_call | solution.py:135
  71.9 1.8 %shard_map.48 = f32[4,1,256,256]{3,2,1,0:T(8,128)S(1)} custom-call(s32[5]{0:T(128)S(1)} %stack.23.sc_ref, bf16[1024,1664]{1,0:T(8,128)(2,1)S(1)} %get-tuple-element.15.dy, bf16[1024,1664]{1,0:T(8,128)(2,1)S(1)} %get-tuple-element.16.dz), custom_call_target="tpu_custom_call" | custom-call | tf_op jit(solution)/shard_map/pallas_call | solution.py:172
  73.7 1.6 %shard_map.47 = f32[4,1,256,256]{3,2,1,0:T(8,128)S(1)} custom-call(s32[5]{0:T(128)S(1)} %stack.23.sc_ref, bf16[1024,1664]{1,0:T(8,128)(2,1)S(1)} %get-tuple-element.15.dy, bf16[1024,1664]{1,0:T(8,128)(2,1)S(1)} %get-tuple-element.16.dz), custom_call_target="tpu_custom_call" | custom-call | tf_op jit(solution)/shard_map/pallas_call | solution.py:172
  75.9 2.7 %shard_map.46.keep = f32[4,2,256,256]{3,2,1,0:T(8,128)S(1)} custom-call(s32[5]{0:T(128)S(1)} %stack.23.sc_ref, bf16[1024,1664]{1,0:T(8,128)(2,1)S(1)} %get-tuple-element.15.dy, bf16[1024,1664]{1,0:T(8,128)(2,1)S(1)} %get-tuple-element.16.dz), custom_call_target="tpu_custom_call" | custom-call | tf_op jit(solution)/shard_map/pallas_call | solution.py:172
  78.6 0.9 collective-permute-done.14.got1
  80.3 0.9 collective-permute-start.16
  81.8 4.8 %collective-permute-start.17 = (bf16[256,256]{1,0:T(8,128)(2,1)S(1)}, bf16[256,256]{1,0:T(8,128)(2,1)S(1)}, u32[]{:S(2)}, u32[]{:S(2)}) collective-permute-start(bf16[256,256]{1,0:T(8,128)(2,1)S(1)} %get-tuple-element.20), channel_id=1, source_target_pairs={{0,6},{2,4},{4,10},{6,8},{8,14},{10,12},{12,2},{14,0},{1,7},{3,5},... | collective-permute-start | bytes 393224 | tf_op jit(solution)/shard_map/ppermute | solution.py:262
  86.7 0.9 collective-permute-start.19
  87.6 2.4 %collective-permute-done.15 = bf16[256,256]{1,0:T(8,128)(2,1)S(1)} collective-permute-done((bf16[256,256]{1,0:T(8,128)(2,1)S(1)}, bf16[256,256]{1,0:T(8,128)(2,1)S(1)}, u32[]{:S(2)}, u32[]{:S(2)}) %collective-permute-start.15) | collective-permute-done | bytes 131104 | tf_op jit(solution)/shard_map/ppermute | solution.py:262
  89.9 3.9 %collective-permute-done.16 = bf16[256,256]{1,0:T(8,128)(2,1)S(1)} collective-permute-done((bf16[256,256]{1,0:T(8,128)(2,1)S(1)}, bf16[256,256]{1,0:T(8,128)(2,1)S(1)}, u32[]{:S(2)}, u32[]{:S(2)}) %collective-permute-start.16) | collective-permute-done | bytes 131104 | tf_op jit(solution)/shard_map/ppermute | solution.py:262
  93.8 2.0 %collective-permute-done.19 = bf16[256,256]{1,0:T(8,128)(2,1)S(1)} collective-permute-done((bf16[256,256]{1,0:T(8,128)(2,1)S(1)}, bf16[256,256]{1,0:T(8,128)(2,1)S(1)}, u32[]{:S(2)}, u32[]{:S(2)}) %collective-permute-start.19) | collective-permute-done | bytes 131104 | tf_op jit(solution)/shard_map/ppermute | solution.py:262
  95.8 3.0 %collective-permute-done.21 = bf16[256,256]{1,0:T(8,128)(2,1)S(1)} collective-permute-done((bf16[256,256]{1,0:T(8,128)(2,1)S(1)}, bf16[256,256]{1,0:T(8,128)(2,1)S(1)}, u32[]{:S(2)}, u32[]{:S(2)}) %collective-permute-start.21) | collective-permute-done | bytes 131104 | tf_op jit(solution)/shard_map/ppermute | solution.py:262
  98.9 2.3 %collective-permute-start.22 = (f32[256,256]{1,0:T(8,128)S(1)}, f32[256,256]{1,0:T(8,128)S(1)}, u32[]{:S(2)}, u32[]{:S(2)}) collective-permute-start(f32[256,256]{1,0:T(8,128)S(1)} %convert_add_fusion), channel_id=1, source_target_pairs={{0,0},{1,16},{2,2},{3,48},{4,4},{5,20},{6,66},{7,52},{8,8},{9,24},... | collective-permute-start | bytes 786440 | tf_op jit(solution)/shard_map/ppermute | solution.py:263
  101.2 9.9 %collective-permute-done.22 = f32[256,256]{1,0:T(8,128)S(1)} collective-permute-done((f32[256,256]{1,0:T(8,128)S(1)}, f32[256,256]{1,0:T(8,128)S(1)}, u32[]{:S(2)}, u32[]{:S(2)}) %collective-permute-start.22) | collective-permute-done | bytes 262176 | tf_op jit(solution)/shard_map/ppermute | solution.py:263
  (35 shorter events, 5.9 us)
Async XLA Ops:
  0.0 36.8 %collective-permute-start.4 = (bf16[1536,128]{1,0:T(8,128)(2,1)}, bf16[1536,128]{1,0:T(8,128)(2,1)S(1)}, u32[]{:S(2)}, u32[]{:S(2)}) collective-permute-start(bf16[1536,128]{1,0:T(8,128)(2,1)} %bitcast.7), channel_id=1, source_target_pairs={{0,48},{16,0},{32,16},{48,32},{1,49},{17,1},{33,17},{49,33},{2,50}... | collective-permute-start | bytes 1179656 | tf_op jit(solution)/shard_map/ppermute | solution.py:244
  5.4 35.5 %collective-permute-start.3 = (bf16[1536,128]{1,0:T(8,128)(2,1)}, bf16[1536,128]{1,0:T(8,128)(2,1)S(1)}, u32[]{:S(2)}, u32[]{:S(2)}) collective-permute-start(bf16[1536,128]{1,0:T(8,128)(2,1)} %bitcast.8), channel_id=1, source_target_pairs={{0,16},{16,32},{32,48},{48,0},{1,17},{17,33},{33,49},{49,1},{2,18}... | collective-permute-start | bytes 1179656 | tf_op jit(solution)/shard_map/ppermute | solution.py:243
  6.1 0.7 copy-start.1
  6.9 0.7 copy-start.2
  7.6 15.4 %collective-permute-start.9 = (bf16[104,128]{1,0:T(8,128)(2,1)S(1)}, bf16[104,128]{1,0:T(8,128)(2,1)S(1)}, u32[]{:S(2)}, u32[]{:S(2)}) collective-permute-start(bf16[104,128]{1,0:T(8,128)(2,1)S(1)} %pack.1.late.m0), channel_id=1, source_target_pairs={{0,48},{16,0},{32,16},{48,32},{1,49},{17,1},{33,17},{49,33},{2,50}... | collective-permute-start | bytes 79880 | tf_op jit(solution)/shard_map/ppermute | solution.py:241
  11.8 11.5 %collective-permute-start.8 = (bf16[104,128]{1,0:T(8,128)(2,1)S(1)}, bf16[104,128]{1,0:T(8,128)(2,1)S(1)}, u32[]{:S(2)}, u32[]{:S(2)}) collective-permute-start(bf16[104,128]{1,0:T(8,128)(2,1)S(1)} %pack.1.late.m0), channel_id=1, source_target_pairs={{0,32},{16,48},{32,0},{48,16},{1,33},{17,49},{33,1},{49,17},{2,34}... | collective-permute-start | bytes 79880 | tf_op jit(solution)/shard_map/ppermute | solution.py:241
  13.2 15.6 %collective-permute-start.7 = (bf16[104,128]{1,0:T(8,128)(2,1)S(1)}, bf16[104,128]{1,0:T(8,128)(2,1)S(1)}, u32[]{:S(2)}, u32[]{:S(2)}) collective-permute-start(bf16[104,128]{1,0:T(8,128)(2,1)S(1)} %pack.1.late.m0), channel_id=1, source_target_pairs={{0,16},{16,32},{32,48},{48,0},{1,17},{17,33},{33,49},{49,1},{2,18}... | collective-permute-start | bytes 79880 | tf_op jit(solution)/shard_map/ppermute | solution.py:241
  29.4 6.4 %collective-permute-start.12 = (bf16[400,128]{1,0:T(8,128)(2,1)S(1)}, bf16[400,128]{1,0:T(8,128)(2,1)S(1)}, u32[]{:S(2)}, u32[]{:S(2)}) collective-permute-start(bf16[400,128]{1,0:T(8,128)(2,1)S(1)} %line.1.s0), channel_id=1, source_target_pairs={{0,192},{64,0},{128,64},{192,128},{1,193},{65,1},{129,65},{193,129... | collective-permute-start | bytes 307208 | tf_op jit(solution)/shard_map/ppermute | solution.py:247
  32.5 28.2 %collective-permute-start.2 = (bf16[1536,128]{1,0:T(8,128)(2,1)}, bf16[1536,128]{1,0:T(8,128)(2,1)S(1)}, u32[]{:S(2)}, u32[]{:S(2)}) collective-permute-start(bf16[1536,128]{1,0:T(8,128)(2,1)} %bitcast.9), channel_id=1, source_target_pairs={{0,192},{64,0},{128,64},{192,128},{1,193},{65,1},{129,65},{193,129... | collective-permute-start | bytes 1179656 | tf_op jit(solution)/shard_map/ppermute | solution.py:245
  33.2 27.5 %collective-permute-start.1 = (bf16[1536,128]{1,0:T(8,128)(2,1)}, bf16[1536,128]{1,0:T(8,128)(2,1)S(1)}, u32[]{:S(2)}, u32[]{:S(2)}) collective-permute-start(bf16[1536,128]{1,0:T(8,128)(2,1)} %bitcast.10), channel_id=1, source_target_pairs={{0,128},{64,192},{128,0},{192,64},{1,129},{65,193},{129,1},{193,65... | collective-permute-start | bytes 1179656 | tf_op jit(solution)/shard_map/ppermute | solution.py:245
  35.8 25.0 %collective-permute-start = (bf16[1536,128]{1,0:T(8,128)(2,1)}, bf16[1536,128]{1,0:T(8,128)(2,1)S(1)}, u32[]{:S(2)}, u32[]{:S(2)}) collective-permute-start(bf16[1536,128]{1,0:T(8,128)(2,1)} %bitcast.11), channel_id=1, source_target_pairs={{0,64},{64,128},{128,192},{192,0},{1,65},{65,129},{129,193},{193,1... | collective-permute-start | bytes 1179656 | tf_op jit(solution)/shard_map/ppermute | solution.py:245
  36.8 19.9 %collective-permute-start.11 = (bf16[400,128]{1,0:T(8,128)(2,1)S(1)}, bf16[400,128]{1,0:T(8,128)(2,1)S(1)}, u32[]{:S(2)}, u32[]{:S(2)}) collective-permute-start(bf16[400,128]{1,0:T(8,128)(2,1)S(1)} %line.1.s0), channel_id=1, source_target_pairs={{0,128},{64,192},{128,0},{192,64},{1,129},{65,193},{129,1},{193,65... | collective-permute-start | bytes 307208 | tf_op jit(solution)/shard_map/ppermute | solution.py:247
  40.9 16.8 %collective-permute-start.10 = (bf16[400,128]{1,0:T(8,128)(2,1)S(1)}, bf16[400,128]{1,0:T(8,128)(2,1)S(1)}, u32[]{:S(2)}, u32[]{:S(2)}) collective-permute-start(bf16[400,128]{1,0:T(8,128)(2,1)S(1)} %line.1.s0), channel_id=1, source_target_pairs={{0,64},{64,128},{128,192},{192,0},{1,65},{65,129},{129,193},{193,1... | collective-permute-start | bytes 307208 | tf_op jit(solution)/shard_map/ppermute | solution.py:247
  56.7 7.4 %collective-permute-start.6 = (bf16[768,128]{1,0:T(8,128)(2,1)S(1)}, bf16[768,128]{1,0:T(8,128)(2,1)S(1)}, u32[]{:S(2)}, u32[]{:S(2)}) collective-permute-start(bf16[768,128]{1,0:T(8,128)(2,1)S(1)} %slice.9), channel_id=1, source_target_pairs={{0,48},{16,0},{32,16},{48,32},{1,49},{17,1},{33,17},{49,33},{2,50}... | collective-permute-start | bytes 589832 | tf_op jit(solution)/shard_map/ppermute | solution.py:249
  57.7 11.0 %collective-permute-start.5 = (bf16[768,128]{1,0:T(8,128)(2,1)S(1)}, bf16[768,128]{1,0:T(8,128)(2,1)S(1)}, u32[]{:S(2)}, u32[]{:S(2)}) collective-permute-start(bf16[768,128]{1,0:T(8,128)(2,1)S(1)} %slice.8), channel_id=1, source_target_pairs={{0,16},{16,32},{32,48},{48,0},{1,17},{17,33},{33,49},{49,1},{2,18}... | collective-permute-start | bytes 589832 | tf_op jit(solution)/shard_map/ppermute | solution.py:248
  59.7 1.0 copy-start
  75.3 3.3 %collective-permute-start.13 = (f32[4,1,256,256]{3,2,1,0:T(8,128)S(1)}, f32[4,1,256,256]{3,2,1,0:T(8,128)S(1)}, u32[]{:S(2)}, u32[]{:S(2)}) collective-permute-start(f32[4,1,256,256]{3,2,1,0:T(8,128)S(1)} %shard_map.47), channel_id=1, source_target_pairs={{0,1},{1,0},{2,3},{3,2},{4,5},{5,4},{6,7},{7,6},{8,9},{9,8},{10,11... | collective-permute-start | bytes 3145736 | tf_op jit(solution)/shard_map/ppermute | solution.py:256
  75.4 4.1 %collective-permute-start.14 = (f32[4,1,256,256]{3,2,1,0:T(8,128)S(1)}, f32[4,1,256,256]{3,2,1,0:T(8,128)S(1)}, u32[]{:S(2)}, u32[]{:S(2)}) collective-permute-start(f32[4,1,256,256]{3,2,1,0:T(8,128)S(1)} %shard_map.48), channel_id=1, source_target_pairs={{0,1},{1,0},{2,3},{3,2},{4,5},{5,4},{6,7},{7,6},{8,9},{9,8},{10,11... | collective-permute-start | bytes 3145736 | tf_op jit(solution)/shard_map/ppermute | solution.py:256
  80.2 9.8 %collective-permute-start.15 = (bf16[256,256]{1,0:T(8,128)(2,1)S(1)}, bf16[256,256]{1,0:T(8,128)(2,1)S(1)}, u32[]{:S(2)}, u32[]{:S(2)}) collective-permute-start(bf16[256,256]{1,0:T(8,128)(2,1)S(1)} %get-tuple-element.18), channel_id=1, source_target_pairs={{0,10},{2,8},{4,14},{6,12},{8,2},{10,0},{12,6},{14,4},{1,11},{3,9}... | collective-permute-start | bytes 393224 | tf_op jit(solution)/shard_map/ppermute | solution.py:262
  80.3 13.6 %collective-permute-start.16 = (bf16[256,256]{1,0:T(8,128)(2,1)S(1)}, bf16[256,256]{1,0:T(8,128)(2,1)S(1)}, u32[]{:S(2)}, u32[]{:S(2)}) collective-permute-start(bf16[256,256]{1,0:T(8,128)(2,1)S(1)} %get-tuple-element.19), channel_id=1, source_target_pairs={{0,8},{2,10},{4,12},{6,14},{8,0},{10,2},{12,4},{14,6},{1,9},{3,11}... | collective-permute-start | bytes 393224 | tf_op jit(solution)/shard_map/ppermute | solution.py:262
  81.8 12.0 %collective-permute-start.17 = (bf16[256,256]{1,0:T(8,128)(2,1)S(1)}, bf16[256,256]{1,0:T(8,128)(2,1)S(1)}, u32[]{:S(2)}, u32[]{:S(2)}) collective-permute-start(bf16[256,256]{1,0:T(8,128)(2,1)S(1)} %get-tuple-element.20), channel_id=1, source_target_pairs={{0,6},{2,4},{4,10},{6,8},{8,14},{10,12},{12,2},{14,0},{1,7},{3,5},... | collective-permute-start | bytes 393224 | tf_op jit(solution)/shard_map/ppermute | solution.py:262
  86.6 7.2 %collective-permute-start.18 = (bf16[256,256]{1,0:T(8,128)(2,1)S(1)}, bf16[256,256]{1,0:T(8,128)(2,1)S(1)}, u32[]{:S(2)}, u32[]{:S(2)}) collective-permute-start(bf16[256,256]{1,0:T(8,128)(2,1)S(1)} %get-tuple-element.21), channel_id=1, source_target_pairs={{0,14},{2,12},{4,2},{6,0},{8,6},{10,4},{12,10},{14,8},{1,15},{3,13... | collective-permute-start | bytes 393224 | tf_op jit(solution)/shard_map/ppermute | solution.py:262
  86.7 9.2 %collective-permute-start.19 = (bf16[256,256]{1,0:T(8,128)(2,1)S(1)}, bf16[256,256]{1,0:T(8,128)(2,1)S(1)}, u32[]{:S(2)}, u32[]{:S(2)}) collective-permute-start(bf16[256,256]{1,0:T(8,128)(2,1)S(1)} %get-tuple-element.22), channel_id=1, source_target_pairs={{0,4},{2,6},{4,8},{6,10},{8,12},{10,14},{12,0},{14,2},{1,5},{3,7},... | collective-permute-start | bytes 393224 | tf_op jit(solution)/shard_map/ppermute | solution.py:262
  89.9 5.9 %collective-permute-start.20 = (bf16[256,256]{1,0:T(8,128)(2,1)S(1)}, bf16[256,256]{1,0:T(8,128)(2,1)S(1)}, u32[]{:S(2)}, u32[]{:S(2)}) collective-permute-start(bf16[256,256]{1,0:T(8,128)(2,1)S(1)} %get-tuple-element.23), channel_id=1, source_target_pairs={{0,12},{2,14},{4,0},{6,2},{8,4},{10,6},{12,8},{14,10},{1,13},{3,15... | collective-permute-start | bytes 393224 | tf_op jit(solution)/shard_map/ppermute | solution.py:262
  93.8 5.0 %collective-permute-start.21 = (bf16[256,256]{1,0:T(8,128)(2,1)S(1)}, bf16[256,256]{1,0:T(8,128)(2,1)S(1)}, u32[]{:S(2)}, u32[]{:S(2)}) collective-permute-start(bf16[256,256]{1,0:T(8,128)(2,1)S(1)} %get-tuple-element.24), channel_id=1, source_target_pairs={{0,2},{2,0},{4,6},{6,4},{8,10},{10,8},{12,14},{14,12},{1,3},{3,1},... | collective-permute-start | bytes 393224 | tf_op jit(solution)/shard_map/ppermute | solution.py:262
  98.9 12.2 %collective-permute-start.22 = (f32[256,256]{1,0:T(8,128)S(1)}, f32[256,256]{1,0:T(8,128)S(1)}, u32[]{:S(2)}, u32[]{:S(2)}) collective-permute-start(f32[256,256]{1,0:T(8,128)S(1)} %convert_add_fusion), channel_id=1, source_target_pairs={{0,0},{1,16},{2,2},{3,48},{4,4},{5,20},{6,66},{7,52},{8,8},{9,24},... | collective-permute-start | bytes 786440 | tf_op jit(solution)/shard_map/ppermute | solution.py:263
